TPU v7x, 32 devices: a whole 2x2x4 slice. The times are simulated.
32 devices in a mesh: dp: 8 (over z, x), tensor: 4 (over y, core).
Axes of the slice: x: 2, y: 2, z: 4, core: 2. Of those that a mesh axis runs over, the one named last changes fastest.
Arguments:
- tokens: bfloat16 [16384, 768], P(('dp', 'tensor')), may hold values from -6 to 6
- w_query: bfloat16 [768, 768], P(None, 'tensor'), may hold values from -0.3125 to 0.3125
- w_key: bfloat16 [768, 768], P(None, 'tensor'), may hold values from -0.3125 to 0.3125
- w_value: bfloat16 [768, 768], P(None, 'tensor'), may hold values from -0.21875 to 0.21875
- b_query: bfloat16 [768], P('tensor'), may hold values from -3 to 3
- b_value: bfloat16 [768], P('tensor'), may hold values from -3 to 3
- w_output: bfloat16 [768, 768], P('tensor'), may hold values from -0.375 to 0.375
- b_output: bfloat16 [768], replicated, may hold values from -3 to 3
- first_gain: bfloat16 [768], replicated, may hold values from 0.5 to 1.5
- first_shift: bfloat16 [768], replicated, may hold values from -3 to 3
- w_up: bfloat16 [768, 3072], P(None, 'tensor'), may hold values from -0.21875 to 0.21875
- b_up: bfloat16 [3072], P('tensor'), may hold values from -3 to 3
- w_down: bfloat16 [3072, 768], P('tensor'), may hold values from -0.15625 to 0.15625
- b_down: bfloat16 [768], replicated, may hold values from -3 to 3
- second_gain: bfloat16 [768], replicated, may hold values from 0.5 to 1.5
- second_shift: bfloat16 [768], replicated, may hold values from -3 to 3
- cotangent: bfloat16 [16384, 768], P(('dp', 'tensor')), may hold values from -24 to 24, as said below
Outputs:
- layer_out: bfloat16 [16384, 768], P(('dp', 'tensor'))
- grad_tokens: bfloat16 [16384, 768], P(('dp', 'tensor'))
- grad_w_query: float32 [768, 768], P(None, 'tensor')
- grad_w_key: float32 [768, 768], P(None, 'tensor')
- grad_w_value: float32 [768, 768], P(None, 'tensor')
- grad_b_query: float32 [768], P('tensor')
- grad_b_value: float32 [768], P('tensor')
- grad_w_output: float32 [768, 768], P('tensor')
- grad_b_output: float32 [768], replicated
- grad_first_gain: float32 [768], replicated
- grad_first_shift: float32 [768], replicated
- grad_w_up: float32 [768, 3072], P(None, 'tensor')
- grad_b_up: float32 [3072], P('tensor')
- grad_w_down: float32 [3072, 768], P('tensor')
- grad_b_down: float32 [768], replicated
- grad_second_gain: float32 [768], replicated
- grad_second_shift: float32 [768], replicated
Inputs may be any that keep to these rules, and one draw needn't show every extreme that they name: cotangent of the layer's output.
All inputs are finite; a program needn't handle non-finite values.
Results may differ from a plain program's by a relative error of at most 0.013.
The roundings to bfloat16 on the way count: a program that leaves them out, or rounds other values in their place, can miss the bound.
Values may be sent and summed in bfloat16 or wider, within the bound.
No kernel may reach another device: no remote copies, remote signals or barrier semaphores. Data moves between devices by JAX's collectives and lax.ppermute only.
A program may use at most 128 MiB of HBM per device.

v0:
```python
import jax
import jax.numpy as jnp
from jax import lax
from jax.sharding import PartitionSpec as P

HEAD = 64
SEQ_LEN = 512


def layer_norm(values, gain_row, shift_row):
    center = values - jnp.mean(values, axis=-1, keepdims=True)
    spread = jnp.mean(center * center, axis=-1, keepdims=True)
    return center * lax.rsqrt(spread + 1e-12) * gain_row + shift_row


def gelu_exact(values):
    return jax.nn.gelu(values, approximate=False)


def contract_rows(left, right):
    return lax.dot_general(
        left, right, (((0,), (0,)), ((), ())), preferred_element_type=jnp.float32
    )


def contract_cols(left, right):
    return lax.dot_general(
        left, right, (((1,), (1,)), ((), ())), preferred_element_type=jnp.float32
    )


def attend_forward(packed):
    queries, key_rows, value_rows = packed
    scores = (
        jnp.einsum("qhd,khd->hqk", queries, key_rows, preferred_element_type=jnp.float32) * 0.125
    )
    highest = jnp.max(scores, axis=-1, keepdims=True)
    unnorm = jnp.exp(scores - highest)
    totals = jnp.sum(unnorm, axis=-1, keepdims=True)
    soft_probs = (unnorm / totals).astype(jnp.bfloat16)
    attended = jnp.einsum(
        "hqk,khd->qhd", soft_probs, value_rows, preferred_element_type=jnp.float32
    )
    return (attended.astype(jnp.bfloat16), highest + jnp.log(totals))


def attend_backward(packed):
    queries, key_rows, value_rows, grad_att, log_total = packed
    scores = (
        jnp.einsum("qhd,khd->hqk", queries, key_rows, preferred_element_type=jnp.float32) * 0.125
    )
    soft_probs = jnp.exp(scores - log_total)
    grad_prob = jnp.einsum("qhd,khd->hqk", grad_att, value_rows, preferred_element_type=jnp.float32)
    inner_sum = jnp.sum(soft_probs * grad_prob, axis=-1, keepdims=True)
    grad_score = (soft_probs * (grad_prob - inner_sum)).astype(jnp.bfloat16)
    grad_query = (
        jnp.einsum("hqk,khd->qhd", grad_score, key_rows, preferred_element_type=jnp.float32) * 0.125
    ).astype(jnp.bfloat16)
    grad_key = (
        jnp.einsum("hqk,qhd->khd", grad_score, queries, preferred_element_type=jnp.float32) * 0.125
    ).astype(jnp.bfloat16)
    grad_value = jnp.einsum(
        "hqk,qhd->khd",
        soft_probs.astype(jnp.bfloat16),
        grad_att,
        preferred_element_type=jnp.float32,
    ).astype(jnp.bfloat16)
    return (grad_query, grad_key, grad_value)


def on_device(
    tokens,
    w_query,
    w_key,
    w_value,
    b_query,
    b_value,
    w_output,
    b_output,
    first_gain,
    first_shift,
    w_up,
    b_up,
    w_down,
    b_down,
    second_gain,
    second_shift,
    cotangent,
):
    share_rows = tokens.shape[0]
    group_rows = share_rows * lax.axis_size("tensor")
    local_width = w_query.shape[1]
    local_heads = local_width // HEAD
    seq_count = group_rows // SEQ_LEN
    w_joined = jnp.concatenate([w_query, w_key, w_value], axis=1)
    b_joined = jnp.concatenate(
        [
            b_query.astype(jnp.float32),
            jnp.zeros((local_width,), jnp.float32),
            b_value.astype(jnp.float32),
        ]
    )

    def split_heads(block):
        return block.reshape(seq_count, SEQ_LEN, local_heads, HEAD)

    inputs_full = lax.all_gather(tokens, "tensor", axis=0, tiled=True)
    projected = (
        jnp.dot(inputs_full, w_joined, preferred_element_type=jnp.float32) + b_joined
    ).astype(jnp.bfloat16)
    queries = split_heads(projected[:, :local_width])
    key_rows = split_heads(projected[:, local_width : 2 * local_width])
    value_rows = split_heads(projected[:, 2 * local_width :])
    attended, log_total = lax.map(attend_forward, (queries, key_rows, value_rows))
    attended = attended.reshape(group_rows, local_width)
    picked = attended
    attention_part = lax.psum_scatter(
        jnp.dot(picked, w_output, preferred_element_type=jnp.float32),
        "tensor",
        scatter_dimension=0,
        tiled=True,
    )
    first_sum = attention_part + b_output.astype(jnp.float32) + tokens.astype(jnp.float32)
    normed, first_pull = jax.vjp(
        layer_norm, first_sum, first_gain.astype(jnp.float32), first_shift.astype(jnp.float32)
    )
    normed_low = normed.astype(jnp.bfloat16)
    normed_full = lax.all_gather(normed_low, "tensor", axis=0, tiled=True)
    up_rows = jnp.dot(normed_full, w_up, preferred_element_type=jnp.float32) + b_up.astype(
        jnp.float32
    )
    active, gelu_pull = jax.vjp(gelu_exact, up_rows)
    active = active.astype(jnp.bfloat16)
    picked = active
    feed_part = lax.psum_scatter(
        jnp.dot(picked, w_down, preferred_element_type=jnp.float32),
        "tensor",
        scatter_dimension=0,
        tiled=True,
    )
    second_sum = feed_part + b_down.astype(jnp.float32) + normed
    layer_out, second_pull = jax.vjp(
        layer_norm, second_sum, second_gain.astype(jnp.float32), second_shift.astype(jnp.float32)
    )
    grad_second, grad_second_gain, grad_second_shift = second_pull(cotangent.astype(jnp.float32))
    grad_b_down = jnp.sum(grad_second, axis=0)
    down_low = grad_second.astype(jnp.bfloat16)
    down_full = lax.all_gather(down_low, "tensor", axis=0, tiled=True)
    grad_w_down = contract_rows(active, down_full)
    grad_active = contract_cols(down_full, w_down)
    grad_up = gelu_pull(grad_active)[0].astype(jnp.bfloat16)
    grad_b_up = jnp.sum(grad_up, axis=0, dtype=jnp.float32)
    grad_w_up = contract_rows(normed_full, grad_up)
    picked = grad_up
    hidden_part = lax.psum_scatter(
        contract_cols(picked, w_up), "tensor", scatter_dimension=0, tiled=True
    )
    grad_normed = hidden_part + grad_second
    grad_first, grad_first_gain, grad_first_shift = first_pull(grad_normed)
    grad_b_output = jnp.sum(grad_first, axis=0)
    first_low = grad_first.astype(jnp.bfloat16)
    first_full = lax.all_gather(first_low, "tensor", axis=0, tiled=True)
    grad_w_output = contract_rows(attended, first_full)
    grad_att = contract_cols(first_full, w_output).astype(jnp.bfloat16)
    grad_query, grad_key, grad_value = lax.map(
        attend_backward, (queries, key_rows, value_rows, split_heads(grad_att), log_total)
    )
    grad_joined = jnp.concatenate(
        [
            grad_query.reshape(group_rows, local_width),
            grad_key.reshape(group_rows, local_width),
            grad_value.reshape(group_rows, local_width),
        ],
        axis=1,
    )
    grad_b_query = jnp.sum(grad_joined[:, :local_width], axis=0, dtype=jnp.float32)
    grad_b_value = jnp.sum(grad_joined[:, 2 * local_width :], axis=0, dtype=jnp.float32)
    grad_w_joined = contract_rows(inputs_full, grad_joined)
    picked = grad_joined
    input_part = lax.psum_scatter(
        contract_cols(picked, w_joined), "tensor", scatter_dimension=0, tiled=True
    )
    grad_tokens = (input_part + grad_first).astype(jnp.bfloat16)
    grad_w_query = grad_w_joined[:, :local_width]
    grad_w_key = grad_w_joined[:, local_width : 2 * local_width]
    grad_w_value = grad_w_joined[:, 2 * local_width :]
    (
        grad_w_query,
        grad_w_key,
        grad_w_value,
        grad_b_query,
        grad_b_value,
        grad_w_output,
        grad_w_up,
        grad_b_up,
        grad_w_down,
    ) = lax.psum(
        (
            grad_w_query,
            grad_w_key,
            grad_w_value,
            grad_b_query,
            grad_b_value,
            grad_w_output,
            grad_w_up,
            grad_b_up,
            grad_w_down,
        ),
        "dp",
    )
    (
        grad_b_output,
        grad_first_gain,
        grad_first_shift,
        grad_b_down,
        grad_second_gain,
        grad_second_shift,
    ) = lax.psum(
        (
            grad_b_output,
            grad_first_gain,
            grad_first_shift,
            grad_b_down,
            grad_second_gain,
            grad_second_shift,
        ),
        ("dp", "tensor"),
    )
    return (
        layer_out.astype(jnp.bfloat16),
        grad_tokens,
        grad_w_query,
        grad_w_key,
        grad_w_value,
        grad_b_query,
        grad_b_value,
        grad_w_output,
        grad_b_output,
        grad_first_gain,
        grad_first_shift,
        grad_w_up,
        grad_b_up,
        grad_w_down,
        grad_b_down,
        grad_second_gain,
        grad_second_shift,
    )


def solution(mesh):
    return jax.shard_map(
        on_device,
        mesh=mesh,
        in_specs=(
            P(("dp", "tensor"), None),
            P(None, "tensor"),
            P(None, "tensor"),
            P(None, "tensor"),
            P("tensor"),
            P("tensor"),
            P("tensor", None),
            P(),
            P(),
            P(),
            P(None, "tensor"),
            P("tensor"),
            P("tensor", None),
            P(),
            P(),
            P(),
            P(("dp", "tensor"), None),
        ),
        out_specs=(
            P(("dp", "tensor"), None),
            P(("dp", "tensor"), None),
            P(None, "tensor"),
            P(None, "tensor"),
            P(None, "tensor"),
            P("tensor"),
            P("tensor"),
            P("tensor", None),
            P(),
            P(),
            P(),
            P(None, "tensor"),
            P("tensor"),
            P("tensor", None),
            P(),
            P(),
            P(),
        ),
        check_vma=False,
    )
```

profile of v0, /device:TPU:0, one launch (start us, length us, event | category | flops | bytes accessed | tf_op | source)
XLA Modules:
  0.0 759.8 jit_solution(11368604049422810197)
XLA Ops:
  12.4 28.5 %all-gather.5.cloned.1.call-done = bf16[2048,768]{1,0:T(8,128)(2,1)} async-done(((bf16[512,768]{1,0:T(8,128)(2,1)}), bf16[2048,768]{1,0:T(8,128)(2,1)}) %all-gather.5.cloned.1.call-update) | async-done | bytes 3145744 | tf_op jit(solution)/shard_map/all_gather | solution.py:107
  40.9 3.9 fusion.63
  54.2 12.9 %while.26 = (s32[]{:T(128)}, bf16[4,512,3,64]{1,3,2,0:T(8,128)(2,1)}, f32[4,3,512,1]{2,1,3,0:T(4,128)}, bf16[4,512,3,64]{1,3,2,0:T(8,128)(2,1)S(1)}, bf16[4,512,...) while((s32[]{:T(128)}, bf16[4,512,3,64]{1,3,2,0:T(8,128)(2,1)}, ...), condition=%wide.region_3.4_spmd, body=%wide.region_0.3_spmd.sunk | while | flops 208501248 | bytes 10281549 | solution.py:114
  70.5 3.7 fusion.78
  74.9 57.8 %reduce-scatter.5.cloned.1.call-done = f32[512,768]{1,0:T(8,128)} async-done(((f32[2048,768]{1,0:T(8,128)}), f32[512,768]{1,0:T(8,128)}) %reduce-scatter.5.cloned.1.call-update) | async-done | bytes 1572880 | tf_op jit(solution)/shard_map/reduce_scatter | solution.py:117
  137.9 27.7 %all-gather.7.cloned.1.call-done = bf16[2048,768]{1,0:T(8,128)(2,1)} async-done(((bf16[512,768]{1,0:T(8,128)(2,1)}), bf16[2048,768]{1,0:T(8,128)(2,1)}) %all-gather.7.cloned.1.call-update) | async-done | bytes 3145744 | tf_op jit(solution)/shard_map/all_gather | solution.py:128
  165.5 18.4 %multiply_convert_fusion.1 = (bf16[2048,768]{1,0:T(8,128)(2,1)S(1)}, f32[2048,768]{1,0:T(8,128)}, f32[2048,768]{1,0:T(8,128)}) fusion(f32[768]{0:T(1024)S(1)} %convert_element_type.116, bf16[2048,768]{1,0:T(8,128)(2,1)} %all-gather.7.cloned.1.call-done, bf16[768,768]{1,0:T(8,128)(2,1)S(1)} %copy-done), kind=kOutput, calls=%fused_computation.64 | convolution fusion | flops 2519728128 | bytes 20057088 | tf_op jit(solution)/shard_map/dot_general | solution.py:129
  185.7 4.5 fusion.79
  193.4 55.3 %reduce-scatter.7.cloned.1.call-done = f32[512,768]{1,0:T(8,128)} async-done(((f32[2048,768]{1,0:T(8,128)}), f32[512,768]{1,0:T(8,128)}) %reduce-scatter.7.cloned.1.call-update) | async-done | bytes 1572880 | tf_op jit(solution)/shard_map/reduce_scatter | solution.py:135
  257.3 28.1 %all-gather.9.cloned.1.call-done = bf16[2048,768]{1,0:T(8,128)(2,1)} async-done(((bf16[512,768]{1,0:T(8,128)(2,1)}), bf16[2048,768]{1,0:T(8,128)(2,1)}) %all-gather.9.cloned.1.call-update) | async-done | bytes 3145744 | tf_op jit(solution)/shard_map/all_gather | solution.py:148
  285.4 11.0 %convert_reduce_fusion = (f32[768]{0:T(1024)}, bf16[2048,768]{1,0:T(8,128)(2,1)S(1)}) fusion(f32[2048,768]{1,0:T(8,128)} %get-tuple-element.195, f32[2048,768]{1,0:T(8,128)} %get-tuple-element.213, f32[768]{0:T(1024)} %copy-done.32, bf16[2048,768]{1,0:T(8,128)(2,1)} %all-gather.9.cloned.1.call-done, bf16[768,768]{1,0:T(8,128)(2,1)} %param.33), kind=kOutput, calls=%fused_computation.62 | convolution fusion | flops 2442657024 | bytes 20060160 | tf_op jit(solution)/shard_map/dot_general | solution.py:27
  298.1 4.5 fusion.80
  302.7 58.5 %reduce-scatter.9.cloned.1.call-done = f32[512,768]{1,0:T(8,128)} async-done(((f32[2048,768]{1,0:T(8,128)}), f32[512,768]{1,0:T(8,128)}) %reduce-scatter.9.cloned.1.call-update) | async-done | bytes 1572880 | tf_op jit(solution)/shard_map/reduce_scatter | solution.py:155
  361.2 3.3 multiply_reduce_fusion.2
  367.7 28.5 %all-gather.11.cloned.1.call-done = bf16[2048,768]{1,0:T(8,128)(2,1)} async-done(((bf16[512,768]{1,0:T(8,128)(2,1)}), bf16[2048,768]{1,0:T(8,128)(2,1)}) %all-gather.11.cloned.1.call-update) | async-done | bytes 3145744 | tf_op jit(solution)/shard_map/all_gather | solution.py:162
  396.2 3.1 convolution_convert_fusion
  402.0 27.8 %while.27 = (s32[]{:T(128)}, bf16[4,512,3,64]{1,3,2,0:T(8,128)(2,1)S(1)}, bf16[4,512,3,64]{1,3,2,0:T(8,128)(2,1)}, bf16[4,512,3,64]{1,3,2,0:T(8,128)(2,1)}, bf16...) while((s32[]{:T(128)}, ...), condition=%wide.region_17.18_spmd, body=%wide.region_15.17_spmd.sunk | while | flops 513243648 | bytes 25611368 | solution.py:165
  435.3 4.6 fusion.81
  440.2 7.0 fusion.84
  447.2 4.2 fusion.83
  457.4 40.8 %all-reduce = (f32[768]{0:T(1024)}, f32[768]{0:T(1024)}, f32[768]{0:T(1024)}, f32[768]{0:T(1024)}, f32[768]{0:T(1024)}, /*index=5*/f32[768]{0:T(1024)}) all-reduce(f32[768]{0:T(1024)S(1)} %get-tuple-element.211, f32[768]{0:T(1024)S(1)} %copy-done.29, f32[768]{0:T(1024)S(1)} %copy-done.30, ...), channel_id=1, replica_groups=mesh['dp'=8,'tensor'=4] {'dp','tensor'}, use_global_device_ids=true, to_apply=%region_28.29 | all-reduce | flops 4608 | bytes 36864 | tf_op jit(solution)/shard_map/psum | solution.py:218
  499.9 22.2 %all-reduce.1 = (f32[192]{0:T(256)}, f32[192]{0:T(256)}, f32[768]{0:T(1024)}) all-reduce(f32[192]{0:T(256)S(1)} %reduce_sum.216, f32[192]{0:T(256)S(1)} %reduce_sum.218, f32[768]{0:T(1024)S(1)} %copy-done.31), channel_id=1, replica_groups=mesh['dp'=8,'tensor'=4] {'dp'}, use_global_device_ids=true, to_apply=%region_23.24 | all-reduce | flops 1152 | bytes 9216 | tf_op jit(solution)/shard_map/psum | solution.py:197
  522.1 2.5 add_convert_fusion.2
  524.6 218.8 %all-reduce.5.cloned.1.call-done = (f32[768,192]{0,1:T(8,128)}, f32[768,192]{0,1:T(8,128)}, f32[768,192]{0,1:T(8,128)}, f32[192,768]{1,0:T(8,128)}, f32[768,768]{1,0:T(8,128)}, /*index=5*/f32[768,768]{1,0:T(8,128)}) async-done(((f32[768,192]{0,1:T(8,128)}, f32[768,192]{0,1:T(8,128)}, f32[768,192]{0,1:T(8,128)}, f32[192,768]{1,0:T(8,128)}, f32[768,768]{1,0:T(8,128)}, /*index=5*/f32[768,768]{1,0:T(8,128)}), ...) | async-done | bytes 7077904 | tf_op jit(solution)/shard_map/psum | solution.py:197
  (218 shorter events, 108.2 us)
Async XLA Ops:
  7.2 158.3 %copy-start = (bf16[768,768]{1,0:T(8,128)(2,1)S(1)}, bf16[768,768]{1,0:T(8,128)(2,1)}, u32[]{:S(2)}) copy-start(bf16[768,768]{1,0:T(8,128)(2,1)} %param.31) | copy-start | bytes 3538948
  7.2 33.7 %all-gather.5.cloned.1.call-start = ((), (), s32[]{:S(2)}) async-start(), calls=%async_computation.4 | async-start | bytes 3932160 | tf_op jit(solution)/shard_map/all_gather | solution.py:107
  7.9 124.8 %reduce-scatter.5.cloned.1.call-start = ((), (), s32[]{:S(2)}) async-start(), calls=%async_computation.5 | async-start | bytes 7864320 | tf_op jit(solution)/shard_map/reduce_scatter | solution.py:117
  12.4 28.5 %copy-start.20 = (bf16[768,576]{0,1:T(8,128)(2,1)}, bf16[768,576]{0,1:T(8,128)(2,1)S(1)}, u32[]{:S(2)}) copy-start(bf16[768,576]{0,1:T(8,128)(2,1)S(1)} %constant_dynamic-update-slice_fusion) | copy-start | bytes 2654212
  67.1 7.1 copy-start.2
  67.1 7.1 copy-start.9
  74.3 91.3 %all-gather.7.cloned.1.call-start = ((), (), s32[]{:S(2)}) async-start(), calls=%async_computation.6 | async-start | bytes 3932160 | tf_op jit(solution)/shard_map/all_gather | solution.py:128
  74.9 61.9 %copy-start.22 = (f32[768]{0:T(1024)}, f32[768]{0:T(1024)S(1)}, u32[]{:S(2)}) copy-start(f32[768]{0:T(1024)S(1)} %convert_element_type.114) | copy-start | bytes 9220
  136.8 111.9 %reduce-scatter.7.cloned.1.call-start = ((), (), s32[]{:S(2)}) async-start(), calls=%async_computation.7 | async-start | bytes 7864320 | tf_op jit(solution)/shard_map/reduce_scatter | solution.py:135
  137.9 46.1 %copy-start.32 = (f32[768]{0:T(1024)}, f32[768]{0:T(1024)S(1)}, u32[]{:S(2)}) copy-start(f32[768]{0:T(1024)S(1)} %convert_element_type.116) | copy-start | bytes 9220
  165.5 20.2 %copy-start.39 = (bf16[768,768]{1,0:T(8,128)(2,1)S(1)}, bf16[768,768]{1,0:T(8,128)(2,1)}, u32[]{:S(2)}) copy-start(bf16[768,768]{1,0:T(8,128)(2,1)} %param.33) | copy-start | bytes 3538948
  190.2 95.3 %all-gather.9.cloned.1.call-start = ((), (), s32[]{:S(2)}) async-start(), calls=%async_computation.8 | async-start | bytes 3932160 | tf_op jit(solution)/shard_map/all_gather | solution.py:148
  256.7 104.5 %reduce-scatter.9.cloned.1.call-start = ((), (), s32[]{:S(2)}) async-start(), calls=%async_computation.9 | async-start | bytes 7864320 | tf_op jit(solution)/shard_map/reduce_scatter | solution.py:155
  302.7 61.8 %copy-start.24 = (f32[512]{0:T(512)S(1)}, f32[512]{0:T(512)}, u32[]{:S(2)}) copy-start(f32[512]{0:T(512)} %copy-done.23) | copy-start | bytes 6148
  302.7 93.5 %all-gather.11.cloned.1.call-start = ((), (), s32[]{:S(2)}) async-start(), calls=%async_computation.10 | async-start | bytes 3932160 | tf_op jit(solution)/shard_map/all_gather | solution.py:162
  364.5 31.7 %copy-start.17 = (bf16[192,768]{1,0:T(8,128)(2,1)S(1)}, bf16[192,768]{1,0:T(8,128)(2,1)}, u32[]{:S(2)}) copy-start(bf16[192,768]{1,0:T(8,128)(2,1)} %param.27) | copy-start | bytes 884740
  367.5 154.6 %reduce-scatter.11.cloned.1.call-start = ((), (), s32[]{:S(2)}) async-start(), calls=%async_computation.11 | async-start | bytes 7864320 | tf_op jit(solution)/shard_map/reduce_scatter | solution.py:180
  439.9 303.6 %all-reduce.5.cloned.1.call-start = ((), (), s32[]{:S(2)}) async-start(), calls=%async_computation.12 | async-start | bytes 14155776 | tf_op jit(solution)/shard_map/psum | solution.py:197
  440.1 7.1 copy-start.38
  440.2 7.1 copy-start.42
  456.7 43.1 %copy-start.31 = (f32[768]{0:T(1024)S(1)}, f32[768]{0:T(1024)}, u32[]{:S(2)}) copy-start(f32[768]{0:T(1024)} %get-tuple-element.185) | copy-start | bytes 9220
  456.7 65.4 %copy-start.5 = (f32[512,768]{1,0:T(8,128)S(1)}, f32[512,768]{1,0:T(8,128)}, u32[]{:S(2)}) copy-start(f32[512,768]{1,0:T(8,128)} %copy-done.4) | copy-start | bytes 4718596
  743.5 5.9 copy-start.15
  743.5 6.7 copy-start.14
  (28 other events, 48.0 us)
Sparse Core Ops, SparseCore 0:
  9.6 31.2 all-gather.4
  74.4 58.3 reduce-scatter.4
  137.0 28.5 all-gather.6
  190.3 58.3 reduce-scatter.6
  256.9 28.5 all-gather.8
  302.8 58.3 reduce-scatter.8
  367.6 28.5 all-gather.10
  440.0 59.7 reduce-scatter.10
  506.0 237.3 all-reduce.4
where the time goes:
time: 768 us; the launch traced here: 760 us
  waiting for transfers between devices  504 us (66%)
  matrix products  98.3 us (13%)
  blocking collectives  63.1 us (8%)
  local copies, waits for them, and re-layouts  46.3 us (6%)
  other arithmetic  31.9 us (4%)
  between operations  14.5 us (2%)
    psum x1, waiting for transfers between devices, on_device(): lax.psum((grad_w_query, grad_w_key, grad_w_value, grad_b_query, grad_b_va...  219 us
    reduce_scatter x1, waiting for transfers between devices, on_device(): lax.psum_scatter(contract_cols(picked, w_up), 'tensor', scatter_dimension...  58.5 us
    reduce_scatter x1, waiting for transfers between devices, on_device(): lax.psum_scatter(jnp.dot(picked, w_output, preferred_element_type=jnp.flo...  57.8 us
    reduce_scatter x1, waiting for transfers between devices, on_device(): lax.psum_scatter(jnp.dot(picked, w_down, preferred_element_type=jnp.float...  55.3 us
    psum x1, blocking collectives, on_device(): lax.psum((grad_b_output, grad_first_gain, grad_first_shift, grad_b_down,...  40.8 us
    all_gather x1, waiting for transfers between devices, on_device(): inputs_full = lax.all_gather(tokens, 'tensor', axis=0, tiled=True)  28.5 us
    all_gather x1, waiting for transfers between devices, on_device(): first_full = lax.all_gather(first_low, 'tensor', axis=0, tiled=True)  28.5 us
    all_gather x1, waiting for transfers between devices, on_device(): down_full = lax.all_gather(down_low, 'tensor', axis=0, tiled=True)  28.1 us
  transfers between devices with their start and end apart: 9, of which 8 were waited for; matrix products, arithmetic and copies ran while one was open for 4% of the time, Pallas kernels for 0%

commit v1 on v0

--- a/solution.py
+++ b/solution.py
@@ -159,7 +159,14 @@
     grad_first, grad_first_gain, grad_first_shift = first_pull(grad_normed)
     grad_b_output = jnp.sum(grad_first, axis=0)
     first_low = grad_first.astype(jnp.bfloat16)
-    first_full = lax.all_gather(first_low, "tensor", axis=0, tiled=True)
+    ring = [first_low]
+    for hop in range(3):
+        ring.append(lax.ppermute(ring[-1], "tensor", [(dev, (dev + 1) % 4) for dev in range(4)]))
+    first_full = jnp.roll(
+        jnp.concatenate(ring[::-1], axis=0),
+        (lax.axis_index("tensor") + 1) * ring[0].shape[0],
+        axis=0,
+    )
     grad_w_output = contract_rows(attended, first_full)
     grad_att = contract_cols(first_full, w_output).astype(jnp.bfloat16)
     grad_query, grad_key, grad_value = lax.map(

time: 768 us -> 776 us (1.010)
    ppermute x0 -> x3, waiting for transfers between devices: none -> 34.3 us  [on_device(): lax.ppermute(ring[-1], 'tensor', [(dev, (dev + 1) % 4) for dev in range(4)])]
    all_gather x1 -> x0, waiting for transfers between devices: 28.5 us -> none  [on_device(): first_full = lax.all_gather(first_low, 'tensor', axis=0, tiled=True)]
    unnamed x100 -> x111, local copies, waits for them, and re-layouts: 23.6 us -> 27.8 us
  transfers between devices with their start and end apart: 9 -> 11, of which waited for: 8 -> 10; matrix products, arithmetic and copies ran while one was open for 4% -> 4% of each run, Pallas kernels for 0% -> 0%
where the time goes in v1:
time: 776 us; the launch traced here: 768 us
  waiting for transfers between devices  511 us (66%)
  matrix products  96.6 us (12%)
  blocking collectives  62.9 us (8%)
  local copies, waits for them, and re-layouts  50.5 us (7%)
  other arithmetic  30.5 us (4%)
  between operations  14.9 us (2%)
    psum x1, waiting for transfers between devices, on_device(): lax.psum((grad_w_query, grad_w_key, grad_w_value, grad_b_query, grad_b_va...  220 us
    reduce_scatter x1, waiting for transfers between devices, on_device(): lax.psum_scatter(contract_cols(picked, w_up), 'tensor', scatter_dimension...  58.5 us
    reduce_scatter x1, waiting for transfers between devices, on_device(): lax.psum_scatter(jnp.dot(picked, w_output, preferred_element_type=jnp.flo...  57.8 us
    reduce_scatter x1, waiting for transfers between devices, on_device(): lax.psum_scatter(jnp.dot(picked, w_down, preferred_element_type=jnp.float...  55.2 us
    psum x1, blocking collectives, on_device(): lax.psum((grad_b_output, grad_first_gain, grad_first_shift, grad_b_down,...  40.5 us
    ppermute x3, waiting for transfers between devices, on_device(): lax.ppermute(ring[-1], 'tensor', [(dev, (dev + 1) % 4) for dev in range(4)])  34.3 us
    all_gather x1, waiting for transfers between devices, on_device(): inputs_full = lax.all_gather(tokens, 'tensor', axis=0, tiled=True)  28.5 us
    all_gather x1, waiting for transfers between devices, on_device(): down_full = lax.all_gather(down_low, 'tensor', axis=0, tiled=True)  28.1 us
  transfers between devices with their start and end apart: 11, of which 10 were waited for; matrix products, arithmetic and copies ran while one was open for 4% of the time, Pallas kernels for 0%

profile of v1, /device:TPU:0, one launch (start us, length us, event | category | flops | bytes accessed | tf_op | source)
XLA Modules:
  0.0 768.1 jit_solution(12621473764738463100)
XLA Ops:
  12.4 28.5 %all-gather.4.cloned.1.call-done = bf16[2048,768]{1,0:T(8,128)(2,1)} async-done(((bf16[512,768]{1,0:T(8,128)(2,1)}), bf16[2048,768]{1,0:T(8,128)(2,1)}) %all-gather.4.cloned.1.call-update) | async-done | bytes 3145744 | tf_op jit(solution)/shard_map/all_gather | solution.py:107
  40.9 3.9 fusion.63
  54.2 12.9 %while.26 = (s32[]{:T(128)}, bf16[4,512,3,64]{1,3,2,0:T(8,128)(2,1)}, f32[4,3,512,1]{2,1,3,0:T(4,128)}, bf16[4,512,3,64]{1,3,2,0:T(8,128)(2,1)S(1)}, bf16[4,512,...) while((s32[]{:T(128)}, bf16[4,512,3,64]{1,3,2,0:T(8,128)(2,1)}, ...), condition=%wide.region_3.4_spmd, body=%wide.region_0.3_spmd.sunk | while | flops 208501248 | bytes 10281049 | solution.py:114
  70.5 3.7 fusion.87
  75.0 57.8 %reduce-scatter.5.cloned.1.call-done = f32[512,768]{1,0:T(8,128)} async-done(((f32[2048,768]{1,0:T(8,128)}), f32[512,768]{1,0:T(8,128)}) %reduce-scatter.5.cloned.1.call-update) | async-done | bytes 1572880 | tf_op jit(solution)/shard_map/reduce_scatter | solution.py:117
  137.9 27.7 %all-gather.6.cloned.1.call-done = bf16[2048,768]{1,0:T(8,128)(2,1)} async-done(((bf16[512,768]{1,0:T(8,128)(2,1)}), bf16[2048,768]{1,0:T(8,128)(2,1)}) %all-gather.6.cloned.1.call-update) | async-done | bytes 3145744 | tf_op jit(solution)/shard_map/all_gather | solution.py:128
  165.5 18.5 %multiply_convert_fusion.1 = (bf16[2048,768]{1,0:T(8,128)(2,1)S(1)}, f32[2048,768]{1,0:T(8,128)}, f32[2048,768]{1,0:T(8,128)}) fusion(f32[768]{0:T(1024)S(1)} %convert_element_type.116, bf16[2048,768]{1,0:T(8,128)(2,1)} %all-gather.6.cloned.1.call-done, bf16[768,768]{1,0:T(8,128)(2,1)S(1)} %copy-done), kind=kOutput, calls=%fused_computation.64 | convolution fusion | flops 2519728128 | bytes 20057088 | tf_op jit(solution)/shard_map/dot_general | solution.py:129
  185.7 4.5 fusion.88
  193.5 55.2 %reduce-scatter.7.cloned.1.call-done = f32[512,768]{1,0:T(8,128)} async-done(((f32[2048,768]{1,0:T(8,128)}), f32[512,768]{1,0:T(8,128)}) %reduce-scatter.7.cloned.1.call-update) | async-done | bytes 1572880 | tf_op jit(solution)/shard_map/reduce_scatter | solution.py:135
  257.4 28.1 %all-gather.8.cloned.1.call-done = bf16[2048,768]{1,0:T(8,128)(2,1)} async-done(((bf16[512,768]{1,0:T(8,128)(2,1)}), bf16[2048,768]{1,0:T(8,128)(2,1)}) %all-gather.8.cloned.1.call-update) | async-done | bytes 3145744 | tf_op jit(solution)/shard_map/all_gather | solution.py:148
  285.5 11.0 %convert_reduce_fusion = (f32[768]{0:T(1024)}, bf16[2048,768]{1,0:T(8,128)(2,1)S(1)}) fusion(f32[2048,768]{1,0:T(8,128)} %get-tuple-element.195, f32[2048,768]{1,0:T(8,128)} %get-tuple-element.213, f32[768]{0:T(1024)} %copy-done.33, bf16[2048,768]{1,0:T(8,128)(2,1)} %all-gather.8.cloned.1.call-done, bf16[768,768]{1,0:T(8,128)(2,1)} %param.33), kind=kOutput, calls=%fused_computation.62 | convolution fusion | flops 2442657024 | bytes 20060160 | tf_op jit(solution)/shard_map/dot_general | solution.py:27
  298.1 4.5 fusion.89
  302.7 58.5 %reduce-scatter.9.cloned.1.call-done = f32[512,768]{1,0:T(8,128)} async-done(((f32[2048,768]{1,0:T(8,128)}), f32[512,768]{1,0:T(8,128)}) %reduce-scatter.9.cloned.1.call-update) | async-done | bytes 1572880 | tf_op jit(solution)/shard_map/reduce_scatter | solution.py:155
  361.2 3.3 multiply_reduce_fusion.2
  366.6 11.4 %collective-permute-done = bf16[512,768]{1,0:T(8,128)(2,1)S(1)} collective-permute-done((bf16[512,768]{1,0:T(8,128)(2,1)S(1)}, bf16[512,768]{1,0:T(8,128)(2,1)S(1)}, u32[]{:S(2)}, u32[]{:S(2)}) %collective-permute-start) | collective-permute-done | bytes 786464 | tf_op jit(solution)/shard_map/ppermute | solution.py:164
  378.0 11.4 %collective-permute-done.1 = bf16[512,768]{1,0:T(8,128)(2,1)S(1)} collective-permute-done((bf16[512,768]{1,0:T(8,128)(2,1)S(1)}, bf16[512,768]{1,0:T(8,128)(2,1)S(1)}, u32[]{:S(2)}, u32[]{:S(2)}) %collective-permute-start.1) | collective-permute-done | bytes 786464 | tf_op jit(solution)/shard_map/ppermute | solution.py:164
  389.6 11.5 %collective-permute-done.2 = bf16[512,768]{1,0:T(8,128)(2,1)} collective-permute-done((bf16[512,768]{1,0:T(8,128)(2,1)S(1)}, bf16[512,768]{1,0:T(8,128)(2,1)}, u32[]{:S(2)}, u32[]{:S(2)}) %collective-permute-start.2) | collective-permute-done | bytes 786464 | tf_op jit(solution)/shard_map/ppermute | solution.py:164
  410.4 27.8 %while.27 = (s32[]{:T(128)}, bf16[4,512,3,64]{1,3,2,0:T(8,128)(2,1)}, bf16[4,512,3,64]{1,3,2,0:T(8,128)(2,1)}, bf16[4,512,3,64]{1,3,2,0:T(8,128)(2,1)S(1)}, bf16...) while((s32[]{:T(128)}, ...), condition=%wide.region_17.18_spmd, body=%wide.region_15.17_spmd.sunk | while | flops 513243648 | bytes 25611376 | solution.py:172
  443.4 4.6 fusion.90
  448.3 7.2 fusion.92
  455.5 4.2 fusion.91
  465.6 40.5 %all-reduce = (f32[768]{0:T(1024)}, f32[768]{0:T(1024)}, f32[768]{0:T(1024)}, f32[768]{0:T(1024)}, f32[768]{0:T(1024)}, /*index=5*/f32[768]{0:T(1024)}) all-reduce(f32[768]{0:T(1024)S(1)} %get-tuple-element.211, f32[768]{0:T(1024)S(1)} %copy-done.30, f32[768]{0:T(1024)S(1)} %copy-done.31, ...), channel_id=1, replica_groups=mesh['dp'=8,'tensor'=4] {'dp','tensor'}, use_global_device_ids=true, to_apply=%region_28.29 | all-reduce | flops 4608 | bytes 36864 | tf_op jit(solution)/shard_map/psum | solution.py:225
  506.6 22.4 %all-reduce.1 = (f32[192]{0:T(256)}, f32[192]{0:T(256)}, f32[768]{0:T(1024)}) all-reduce(f32[192]{0:T(256)S(1)} %reduce_sum.216, f32[192]{0:T(256)S(1)} %reduce_sum.218, f32[768]{0:T(1024)S(1)} %copy-done.32), channel_id=1, replica_groups=mesh['dp'=8,'tensor'=4] {'dp'}, use_global_device_ids=true, to_apply=%region_23.24 | all-reduce | flops 1152 | bytes 9216 | tf_op jit(solution)/shard_map/psum | solution.py:204
  531.5 220.0 %all-reduce.5.cloned.1.call-done = (f32[768,192]{0,1:T(8,128)}, f32[768,192]{0,1:T(8,128)}, f32[768,192]{0,1:T(8,128)}, f32[192,768]{1,0:T(8,128)}, f32[768,768]{1,0:T(8,128)}, /*index=5*/f32[768,768]{1,0:T(8,128)}) async-done(((f32[768,192]{0,1:T(8,128)}, f32[768,192]{0,1:T(8,128)}, f32[768,192]{0,1:T(8,128)}, f32[192,768]{1,0:T(8,128)}, f32[768,768]{1,0:T(8,128)}, /*index=5*/f32[768,768]{1,0:T(8,128)}), ...) | async-done | bytes 7077904 | tf_op jit(solution)/shard_map/psum | solution.py:204
  (234 shorter events, 114.8 us)
Async XLA Ops:
  7.2 158.4 %copy-start = (bf16[768,768]{1,0:T(8,128)(2,1)S(1)}, bf16[768,768]{1,0:T(8,128)(2,1)}, u32[]{:S(2)}) copy-start(bf16[768,768]{1,0:T(8,128)(2,1)} %param.31) | copy-start | bytes 3538948
  7.2 33.7 %all-gather.4.cloned.1.call-start = ((), (), s32[]{:S(2)}) async-start(), calls=%async_computation.4 | async-start | bytes 3932160 | tf_op jit(solution)/shard_map/all_gather | solution.py:107
  7.9 124.9 %reduce-scatter.5.cloned.1.call-start = ((), (), s32[]{:S(2)}) async-start(), calls=%async_computation.5 | async-start | bytes 7864320 | tf_op jit(solution)/shard_map/reduce_scatter | solution.py:117
  12.4 28.5 %copy-start.21 = (bf16[768,576]{0,1:T(8,128)(2,1)}, bf16[768,576]{0,1:T(8,128)(2,1)S(1)}, u32[]{:S(2)}) copy-start(bf16[768,576]{0,1:T(8,128)(2,1)S(1)} %constant_dynamic-update-slice_fusion) | copy-start | bytes 2654212
  67.1 7.1 copy-start.11
  74.3 91.3 %all-gather.6.cloned.1.call-start = ((), (), s32[]{:S(2)}) async-start(), calls=%async_computation.6 | async-start | bytes 3932160 | tf_op jit(solution)/shard_map/all_gather | solution.py:128
  74.9 61.9 %copy-start.23 = (f32[768]{0:T(1024)}, f32[768]{0:T(1024)S(1)}, u32[]{:S(2)}) copy-start(f32[768]{0:T(1024)S(1)} %convert_element_type.114) | copy-start | bytes 9220
  136.9 111.9 %reduce-scatter.7.cloned.1.call-start = ((), (), s32[]{:S(2)}) async-start(), calls=%async_computation.7 | async-start | bytes 7864320 | tf_op jit(solution)/shard_map/reduce_scatter | solution.py:135
  137.9 46.1 %copy-start.33 = (f32[768]{0:T(1024)}, f32[768]{0:T(1024)S(1)}, u32[]{:S(2)}) copy-start(f32[768]{0:T(1024)S(1)} %convert_element_type.116) | copy-start | bytes 9220
  165.5 20.2 %copy-start.39 = (bf16[768,768]{1,0:T(8,128)(2,1)S(1)}, bf16[768,768]{1,0:T(8,128)(2,1)}, u32[]{:S(2)}) copy-start(bf16[768,768]{1,0:T(8,128)(2,1)} %param.33) | copy-start | bytes 3538948
  190.2 95.3 %all-gather.8.cloned.1.call-start = ((), (), s32[]{:S(2)}) async-start(), calls=%async_computation.8 | async-start | bytes 3932160 | tf_op jit(solution)/shard_map/all_gather | solution.py:148
  256.8 104.4 %reduce-scatter.9.cloned.1.call-start = ((), (), s32[]{:S(2)}) async-start(), calls=%async_computation.9 | async-start | bytes 7864320 | tf_op jit(solution)/shard_map/reduce_scatter | solution.py:155
  302.7 61.8 %copy-start.25 = (f32[512]{0:T(512)S(1)}, f32[512]{0:T(512)}, u32[]{:S(2)}) copy-start(f32[512]{0:T(512)} %copy-done.24) | copy-start | bytes 6148
  302.7 226.3 %reduce-scatter.11.cloned.1.call-start = ((), (), s32[]{:S(2)}) async-start(), calls=%async_computation.10 | async-start | bytes 7864320 | tf_op jit(solution)/shard_map/reduce_scatter | solution.py:187
  366.5 11.5 %collective-permute-start = (bf16[512,768]{1,0:T(8,128)(2,1)S(1)}, bf16[512,768]{1,0:T(8,128)(2,1)S(1)}, u32[]{:S(2)}, u32[]{:S(2)}) collective-permute-start(bf16[512,768]{1,0:T(8,128)(2,1)S(1)} %get-tuple-element.212), channel_id=1, source_target_pairs={{0,1},{1,2},{2,3},{3,0},{4,5},{5,6},{6,7},{7,4},{8,9},{9,10},{10,1... | collective-permute-start | bytes 2359304 | tf_op jit(solution)/shard_map/ppermute | solution.py:164
  378.0 11.4 %collective-permute-start.1 = (bf16[512,768]{1,0:T(8,128)(2,1)S(1)}, bf16[512,768]{1,0:T(8,128)(2,1)S(1)}, u32[]{:S(2)}, u32[]{:S(2)}) collective-permute-start(bf16[512,768]{1,0:T(8,128)(2,1)S(1)} %collective-permute-done), channel_id=1, source_target_pairs={{0,1},{1,2},{2,3},{3,0},{4,5},{5,6},{6,7},{7,4},{8,9},{9,10},{10,1... | collective-permute-start | bytes 2359304 | tf_op jit(solution)/shard_map/ppermute | solution.py:164
  389.4 11.7 %collective-permute-start.2 = (bf16[512,768]{1,0:T(8,128)(2,1)S(1)}, bf16[512,768]{1,0:T(8,128)(2,1)}, u32[]{:S(2)}, u32[]{:S(2)}) collective-permute-start(bf16[512,768]{1,0:T(8,128)(2,1)S(1)} %collective-permute-done.1), channel_id=1, source_target_pairs={{0,1},{1,2},{2,3},{3,0},{4,5},{5,6},{6,7},{7,4},{8,9},{9,10},{10,1... | collective-permute-start | bytes 2359304 | tf_op jit(solution)/shard_map/ppermute | solution.py:164
  448.0 303.5 %all-reduce.5.cloned.1.call-start = ((), (), s32[]{:S(2)}) async-start(), calls=%async_computation.11 | async-start | bytes 14155776 | tf_op jit(solution)/shard_map/psum | solution.py:204
  448.2 7.2 copy-start.38
  448.2 7.2 copy-start.42
  448.3 11.4 %slice-start = ((s8[6291456]{0:T(1024)(128)(4,1)}), s8[4194304]{0:T(1024)(128)(4,1)S(1)}, s32[]{:S(2)}) async-start(s8[6291456]{0:T(1024)(128)(4,1)} %bitcast.164), calls=%async_computation.12 | async-start | bytes 8388608
  464.9 41.3 %copy-start.10 = (bf16[4,512,3,64]{1,3,2,0:T(8,128)(2,1)S(1)}, bf16[4,512,3,64]{1,3,2,0:T(8,128)(2,1)}, u32[]{:S(2)}) copy-start(bf16[4,512,3,64]{1,3,2,0:T(8,128)(2,1)} %get-tuple-element.101) | copy-start | bytes 2359300
  464.9 41.7 %copy-start.32 = (f32[768]{0:T(1024)S(1)}, f32[768]{0:T(1024)}, u32[]{:S(2)}) copy-start(f32[768]{0:T(1024)} %get-tuple-element.185) | copy-start | bytes 9220
  464.9 64.1 %copy-start.5 = (f32[512,768]{1,0:T(8,128)S(1)}, f32[512,768]{1,0:T(8,128)}, u32[]{:S(2)}) copy-start(f32[512,768]{1,0:T(8,128)} %copy-done.4) | copy-start | bytes 4718596
  (32 other events, 75.9 us)
Sparse Core Ops, SparseCore 0:
  9.6 31.2 all-gather.3
  74.4 58.3 reduce-scatter.4
  137.0 28.5 all-gather.5
  190.3 58.3 reduce-scatter.6
  256.9 28.5 all-gather.7
  302.8 58.3 reduce-scatter.8
  448.1 59.7 reduce-scatter.10
  514.1 237.2 all-reduce.4
